TPU v7x, 128 devices: a whole 4x4x4 slice. The times are simulated.
128 devices in a mesh: dp: 32 (over x, z, y_lo), mp: 4 (over y_hi, core).
Axes of the slice: x: 4, y: 4 (y_hi: 2, y_lo: 2; y = y_hi * 2 + y_lo), z: 4, core: 2. Of those that a mesh axis runs over, the one named last changes fastest.
Arguments:
- inputs: bfloat16 [12288, 8192], P('dp', 'mp'), may hold values from -6 to 6
- gate_preact: bfloat16 [12288, 28672], P('dp', 'mp'), may hold values from -6 to 6
- hidden_grad: bfloat16 [12288, 28672], P('dp', 'mp'), may hold values from -0.109375 to 0.109375
- projector: bfloat16 [8192, 512], P('mp'), may hold values from -0.0625 to 0.0625
- first_moment: float32 [28672, 512], P(('mp', 'dp')), may hold values from -0.6 to 0.6
- second_moment: float32 [28672, 512], P(('mp', 'dp')), may hold values from 0.01 to 0.1
Outputs:
- new_first: float32 [28672, 512], P(('mp', 'dp'))
- new_second: float32 [28672, 512], P(('mp', 'dp'))
- weight_update: bfloat16 [28672, 8192], P(('mp', 'dp'))
All inputs are finite; a program needn't handle non-finite values.
Results may differ from a plain program's by a relative error of at most 0.0058.
Values may be sent and summed in bfloat16 or wider, within the bound.
No kernel may reach another device: no remote copies, remote signals or barrier semaphores. Data moves between devices by JAX's collectives and lax.ppermute only.
A program may use at most 128 MiB of HBM per device.

v0:
```python
import jax
import jax.numpy as jnp
from jax import lax
from jax.sharding import PartitionSpec as P


def local(inputs, gate_preact, hidden_grad, projector, first_moment, second_moment):
    grad_up = (
        hidden_grad.astype(jnp.float32) * jax.nn.silu(gate_preact.astype(jnp.float32))
    ).astype(jnp.bfloat16)
    full_proj = lax.all_gather(projector, "mp", axis=0, tiled=True)
    coord_sum = jnp.dot(
        lax.all_gather(inputs, "mp", axis=1, tiled=True),
        full_proj,
        preferred_element_type=jnp.float32,
    )
    coords = coord_sum.astype(jnp.bfloat16)
    projected = lax.psum_scatter(
        lax.dot_general(
            grad_up, coords, (((0,), (0,)), ((), ())), preferred_element_type=jnp.float32
        ),
        "dp",
        scatter_dimension=0,
        tiled=True,
    )
    new_first = 0.9 * first_moment + 0.1 * projected
    new_second = 0.95 * second_moment + 0.05 * projected * projected
    direction = new_first / (1.0 - 0.81) / (jnp.sqrt(new_second / (1.0 - 0.9025)) + 1e-08)
    direction = direction.astype(jnp.bfloat16)
    update = 4.0 * lax.dot_general(
        direction, full_proj, (((1,), (1,)), ((), ())), preferred_element_type=jnp.float32
    )
    return (new_first, new_second, update.astype(jnp.bfloat16))


def solution(mesh):
    return jax.shard_map(
        local,
        mesh=mesh,
        in_specs=(
            P("dp", "mp"),
            P("dp", "mp"),
            P("dp", "mp"),
            P("mp", None),
            P(("mp", "dp"), None),
            P(("mp", "dp"), None),
        ),
        out_specs=(P(("mp", "dp"), None), P(("mp", "dp"), None), P(("mp", "dp"), None)),
        check_vma=False,
    )
```

profile of v0, /device:TPU:74, one launch (start us, length us, event | category | flops | bytes accessed | tf_op | source)
XLA Modules:
  0.0 480.9 jit_solution(11658029528777716738)
XLA Ops:
  7.2 0.0 all-gather.3.cloned.1.call-start
  7.2 0.7 all-gather.3.cloned.1.call-update
  7.9 0.0 all-gather.5.cloned.1.call-start
  7.9 0.7 all-gather.5.cloned.1.call-update
  8.6 0.0 reduce-scatter.2.cloned.1.call-start
  8.7 52.0 %all-gather.3.cloned.1.call-done = bf16[384,8192]{1,0:T(8,128)(2,1)} async-done(((bf16[384,2048]{1,0:T(8,128)(2,1)}), bf16[384,8192]{1,0:T(8,128)(2,1)}) %all-gather.3.cloned.1.call-update) | async-done | bytes 6291472 | tf_op jit(solution)/shard_map/all_gather | solution.py:13
  60.7 63.4 %all-gather.5.cloned.1.call-done = bf16[8192,512]{1,0:T(8,128)(2,1)} async-done(((bf16[2048,512]{1,0:T(8,128)(2,1)}), bf16[8192,512]{1,0:T(8,128)(2,1)}) %all-gather.5.cloned.1.call-update) | async-done | bytes 8388624 | tf_op jit(solution)/shard_map/all_gather | solution.py:11
  124.1 21.4 %fusion.6 = f32[7168,512]{1,0:T(8,128)} fusion(bf16[384,7168]{1,0:T(8,128)(2,1)} %param.7, bf16[384,7168]{1,0:T(8,128)(2,1)} %param.8, bf16[384,8192]{1,0:T(8,128)(2,1)} %all-gather.3.cloned.1.call-done, bf16[8192,512]{1,0:T(8,128)(2,1)} %all-gather.5.cloned.1.call-done), kind=kOutput, calls=%fused_computation.9 | convolution fusion | flops 6062014464 | bytes 40370176 | tf_op jit(solution)/shard_map/dot_general | solution.py:19
  145.5 0.0 copy-start
  145.5 0.0 copy-start.1
  145.5 0.0 reduce-scatter.2.cloned.1.call-update
  145.5 319.3 %reduce-scatter.2.cloned.1.call-done = f32[224,512]{1,0:T(8,128)} async-done(((f32[7168,512]{1,0:T(8,128)}), f32[224,512]{1,0:T(8,128)}) %reduce-scatter.2.cloned.1.call-update) | async-done | bytes 458768 | tf_op jit(solution)/shard_map/reduce_scatter | solution.py:18
  464.8 0.0 copy-done
  464.8 0.0 copy-done.1
  464.8 1.2 fusion.8
  466.0 0.0 copy-start.2
  466.0 0.0 copy-start.3
  466.0 8.3 %fusion.5 = bf16[224,8192]{1,0:T(8,128)(2,1)} fusion(bf16[8192,512]{1,0:T(8,128)(2,1)} %all-gather.5.cloned.1.call-done, f32[224,512]{1,0:T(8,128)S(1)} %get-tuple-element.3, f32[224,512]{1,0:T(8,128)S(1)} %get-tuple-element.4), kind=kOutput, calls=%fused_computation.8 | convolution fusion | flops 1883291648 | bytes 12976128 | tf_op jit(solution)/shard_map/dot_general | solution.py:30
  474.3 0.0 copy-done.2
  474.3 0.0 copy-done.3
Async XLA Ops:
  7.2 53.6 %all-gather.3.cloned.1.call-start = ((), (), s32[]{:S(2)}) async-start(), calls=%async_computation.1 | async-start | bytes 7864320 | tf_op jit(solution)/shard_map/all_gather | solution.py:13
  7.9 116.2 %all-gather.5.cloned.1.call-start = ((), (), s32[]{:S(2)}) async-start(), calls=%async_computation.2 | async-start | bytes 10485760 | tf_op jit(solution)/shard_map/all_gather | solution.py:11
  8.6 456.1 %reduce-scatter.2.cloned.1.call-start = ((), (), s32[]{:S(2)}) async-start(), calls=%async_computation.3 | async-start | bytes 15138816 | tf_op jit(solution)/shard_map/reduce_scatter | solution.py:18
  145.5 319.3 %copy-start = (f32[224,512]{1,0:T(8,128)S(1)}, f32[224,512]{1,0:T(8,128)}, u32[]{:S(2)}) copy-start(f32[224,512]{1,0:T(8,128)} %param.11) | copy-start | bytes 1376260
  145.5 319.3 %copy-start.1 = (f32[224,512]{1,0:T(8,128)S(1)}, f32[224,512]{1,0:T(8,128)}, u32[]{:S(2)}) copy-start(f32[224,512]{1,0:T(8,128)} %param.10) | copy-start | bytes 1376260
  466.0 8.4 %copy-start.2 = (f32[224,512]{1,0:T(8,128)}, f32[224,512]{1,0:T(8,128)S(1)}, u32[]{:S(2)}) copy-start(f32[224,512]{1,0:T(8,128)S(1)} %get-tuple-element.3) | copy-start | bytes 1376260
  466.0 8.3 %copy-start.3 = (f32[224,512]{1,0:T(8,128)}, f32[224,512]{1,0:T(8,128)S(1)}, u32[]{:S(2)}) copy-start(f32[224,512]{1,0:T(8,128)S(1)} %get-tuple-element.4) | copy-start | bytes 1376260
Sparse Core Ops, SparseCore 0:
  9.6 51.0 all-gather.2
  62.4 61.6 all-gather.4
  145.6 319.0 reduce-scatter.1
where the time goes:
time: 481 us
  waiting for transfers between devices  436 us (91%)
  matrix products  29.7 us (6%)
  between operations  13.8 us (3%)
    reduce_scatter x1, waiting for transfers between devices, local(): lax.psum_scatter(lax.dot_general(grad_up, coords, (((0,), (0,)), ((), ())...  319 us
    all_gather x1, waiting for transfers between devices, local(): full_proj = lax.all_gather(projector, 'mp', axis=0, tiled=True)  63.4 us
    all_gather x1, waiting for transfers between devices, local(): lax.all_gather(inputs, 'mp', axis=1, tiled=True)  52 us
    dot_general x1, matrix products, local(): lax.dot_general(grad_up, coords, (((0,), (0,)), ((), ())), preferred_elem...  21.4 us
  transfers between devices with their start and end apart: 3, of which 3 were waited for; matrix products, arithmetic and copies ran while one was open for 0% of the time, Pallas kernels for 0%

commit v1 on v0

--- a/solution.py
+++ b/solution.py
@@ -8,7 +8,9 @@
     grad_up = (
         hidden_grad.astype(jnp.float32) * jax.nn.silu(gate_preact.astype(jnp.float32))
     ).astype(jnp.bfloat16)
-    full_proj = lax.all_gather(projector, "mp", axis=0, tiled=True)
+    full_proj = jnp.concatenate(
+        lax.all_to_all(jnp.stack([projector] * lax.axis_size("mp")), "mp", 0, 0), axis=0
+    )
     coord_sum = jnp.dot(
         lax.all_gather(inputs, "mp", axis=1, tiled=True),
         full_proj,

time: 481 us -> 499 us (1.037)
  blocking collectives: 0 us -> 132 us
  waiting for transfers between devices: 436 us -> 320 us
    all_to_all x0 -> x1, blocking collectives: none -> 132 us  [local(): lax.all_to_all(jnp.stack([projector] * lax.axis_size('mp')), 'mp', 0, 0)]
    all_gather x1 -> x0, waiting for transfers between devices: 63.4 us -> none  [local(): full_proj = lax.all_gather(projector, 'mp', axis=0, tiled=True)]
    all_gather x1, waiting for transfers between devices: 52 us -> 0.01 us  [local(): lax.all_gather(inputs, 'mp', axis=1, tiled=True)]
  transfers between devices with their start and end apart: 3 -> 2, of which waited for: 3 -> 1; matrix products, arithmetic and copies ran while one was open for 0% -> 0% of each run, Pallas kernels for 0% -> 0%
where the time goes in v1:
time: 499 us
  waiting for transfers between devices  320 us (64%)
  blocking collectives  132 us (26%)
  matrix products  29.7 us (6%)
  between operations  14.1 us (3%)
    reduce_scatter x1, waiting for transfers between devices, local(): lax.psum_scatter(lax.dot_general(grad_up, coords, (((0,), (0,)), ((), ())...  319 us
    all_to_all x1, blocking collectives, local(): lax.all_to_all(jnp.stack([projector] * lax.axis_size('mp')), 'mp', 0, 0)  132 us
    dot_general x1, matrix products, local(): lax.dot_general(grad_up, coords, (((0,), (0,)), ((), ())), preferred_elem...  21.4 us
  transfers between devices with their start and end apart: 2, of which 1 were waited for; matrix products, arithmetic and copies ran while one was open for 0% of the time, Pallas kernels for 0%

profile of v1, /device:TPU:74, one launch (start us, length us, event | category | flops | bytes accessed | tf_op | source)
XLA Modules:
  0.0 498.9 jit_solution(9497055564627135242)
XLA Ops:
  7.2 0.0 all-gather.2.cloned.1.call-start
  7.2 0.7 all-gather.2.cloned.1.call-update
  7.9 0.0 reduce-scatter.2.cloned.1.call-start
  7.9 2.3 stack.2
  10.2 132.0 %all_to_all.5 = bf16[4,2048,512]{2,1,0:T(8,128)(2,1)} all-to-all(bf16[4,2048,512]{2,1,0:T(8,128)(2,1)S(1)} %stack.2), channel_id=1, replica_groups=mesh['dp'=32,'mp'=4] {'mp'}, dimensions={0} | all-to-all | bytes 16777216 | tf_op jit(solution)/shard_map/all_to_all | solution.py:12
  142.2 0.0 all-gather.2.cloned.1.call-done
  142.2 21.4 %fusion.6 = f32[7168,512]{1,0:T(8,128)} fusion(bf16[384,7168]{1,0:T(8,128)(2,1)} %param.7, bf16[384,7168]{1,0:T(8,128)(2,1)} %param.8, bf16[384,8192]{1,0:T(8,128)(2,1)} %all-gather.2.cloned.1.call-done, bf16[8192,512]{1,0:T(8,128)(2,1)} %bitcast.4), kind=kOutput, calls=%fused_computation.9 | convolution fusion | flops 6062014464 | bytes 40370176 | tf_op jit(solution)/shard_map/dot_general | solution.py:21
  163.6 0.0 copy-start
  163.6 0.0 copy-start.1
  163.6 0.0 reduce-scatter.2.cloned.1.call-update
  163.6 318.9 %reduce-scatter.2.cloned.1.call-done = f32[224,512]{1,0:T(8,128)} async-done(((f32[7168,512]{1,0:T(8,128)}), f32[224,512]{1,0:T(8,128)}) %reduce-scatter.2.cloned.1.call-update) | async-done | bytes 458768 | tf_op jit(solution)/shard_map/reduce_scatter | solution.py:20
  482.5 0.0 copy-done
  482.5 0.0 copy-done.1
  482.5 1.2 fusion.8
  483.7 0.0 copy-start.2
  483.7 0.0 copy-start.3
  483.7 8.3 %fusion.5 = bf16[224,8192]{1,0:T(8,128)(2,1)} fusion(bf16[8192,512]{1,0:T(8,128)(2,1)} %bitcast.5, f32[224,512]{1,0:T(8,128)S(1)} %get-tuple-element.3, f32[224,512]{1,0:T(8,128)S(1)} %get-tuple-element.4), kind=kOutput, calls=%fused_computation.8 | convolution fusion | flops 1883291648 | bytes 12976128 | tf_op jit(solution)/shard_map/dot_general | solution.py:32
  492.0 0.0 copy-done.2
  492.0 0.0 copy-done.3
Async XLA Ops:
  7.2 135.1 %all-gather.2.cloned.1.call-start = ((), (), s32[]{:S(2)}) async-start(), calls=%async_computation.2 | async-start | bytes 7864320 | tf_op jit(solution)/shard_map/all_gather | solution.py:15
  7.9 474.6 %reduce-scatter.2.cloned.1.call-start = ((), (), s32[]{:S(2)}) async-start(), calls=%async_computation.3 | async-start | bytes 15138816 | tf_op jit(solution)/shard_map/reduce_scatter | solution.py:20
  163.6 318.9 %copy-start = (f32[224,512]{1,0:T(8,128)S(1)}, f32[224,512]{1,0:T(8,128)}, u32[]{:S(2)}) copy-start(f32[224,512]{1,0:T(8,128)} %param.11) | copy-start | bytes 1376260
  163.6 318.9 %copy-start.1 = (f32[224,512]{1,0:T(8,128)S(1)}, f32[224,512]{1,0:T(8,128)}, u32[]{:S(2)}) copy-start(f32[224,512]{1,0:T(8,128)} %param.10) | copy-start | bytes 1376260
  483.7 8.4 %copy-start.2 = (f32[224,512]{1,0:T(8,128)}, f32[224,512]{1,0:T(8,128)S(1)}, u32[]{:S(2)}) copy-start(f32[224,512]{1,0:T(8,128)S(1)} %get-tuple-element.3) | copy-start | bytes 1376260
  483.7 8.3 %copy-start.3 = (f32[224,512]{1,0:T(8,128)}, f32[224,512]{1,0:T(8,128)S(1)}, u32[]{:S(2)}) copy-start(f32[224,512]{1,0:T(8,128)S(1)} %get-tuple-element.4) | copy-start | bytes 1376260
Sparse Core Ops, SparseCore 0:
  9.6 84.8 all-gather.1
  163.8 318.6 reduce-scatter.1
